TPU v7x, 256 devices: a whole 4x4x8 slice. The times are simulated.
256 devices in a mesh: samp: 16 (over z, core), feat: 16 (over x, y).
Axes of the slice: x: 4, y: 4, z: 8, core: 2. Of those that a mesh axis runs over, the one named last changes fastest.
Arguments:
- differences: bfloat16 [9216, 131072], P('samp', 'feat'), may hold values from -600 to 600
- start_block: bfloat16 [64, 131072], P(None, 'feat'), may hold values from -6 to 6
Outputs:
- directions: float32 [64, 131072], P(None, 'feat')
- layer_scores: float32 [16, 64], P('feat')
All inputs are finite; a program needn't handle non-finite values.
Results may differ from a plain program's by a relative error of at most 0.0043.
Values may be sent and summed in bfloat16 or wider, within the bound.
A program may use at most 64 MiB of HBM per device.

v0:
```python
import math
import jax
import jax.numpy as jnp
from jax import lax
from jax.sharding import PartitionSpec as P

WIDTH = 8192
ITERS = 2
FEATURES = 131072


def orthonormal(pulled, gram):
    lower = jnp.linalg.cholesky(gram)
    return lax.linalg.triangular_solve(lower, pulled, left_side=True, lower=True)


def on_device(differences, start_block):
    block = start_block
    basis = None
    for step in range(ITERS):
        partial_rows = lax.dot_general(
            block, differences, (((1,), (1,)), ((), ())), preferred_element_type=jnp.float32
        )
        projected = lax.psum(partial_rows, "feat").astype(jnp.bfloat16)
        partial_cols = jnp.dot(projected, differences, preferred_element_type=jnp.float32)
        pulled = lax.psum(partial_cols, "samp")
        local_gram = jnp.dot(pulled, pulled.T, precision=lax.Precision.HIGHEST)
        gram = lax.psum(local_gram, "feat")
        basis = orthonormal(pulled, gram)
        block = basis.astype(jnp.bfloat16)
    directions = basis * math.sqrt(FEATURES)
    samples = differences.shape[0]
    layers_here = differences.shape[1] // WIDTH
    stacked = differences.reshape(samples, layers_here, WIDTH)
    block_layers = block.reshape(block.shape[0], layers_here, WIDTH)
    along = jnp.einsum("kjw,sjw->jks", block_layers, stacked, preferred_element_type=jnp.float32)
    captured = jnp.sum(along * along, axis=2)
    energy = jnp.einsum("sjw,sjw->j", stacked, stacked, preferred_element_type=jnp.float32)
    captured, energy = lax.psum((captured, energy), "samp")
    layer_scores = FEATURES * captured / (energy[:, None] + 1e-06)
    return (directions, layer_scores)


def solution(mesh):
    in_specs = (P("samp", "feat"), P(None, "feat"))
    out_specs = (P(None, "feat"), P("feat", None))
    return jax.shard_map(
        on_device, mesh=mesh, in_specs=in_specs, out_specs=out_specs, check_vma=False
    )
```

profile of v0, /device:TPU:1, one launch (start us, length us, event | category | flops | bytes accessed | tf_op | source)
XLA Modules:
  0.0 635.0 jit_solution(9600654586622632830)
XLA Ops:
  7.2 0.0 copy-start
  7.2 0.0 all-reduce.6.cloned.1.call-start
  7.2 1.2 copy-done
  8.4 6.6 %fusion.16 = f32[64,576]{1,0:T(8,128)S(1)} fusion(bf16[64,8192]{1,0:T(8,128)(2,1)S(1)} %copy-done, bf16[576,8192]{1,0:T(8,128)(2,1)} %param.5), kind=kOutput, calls=%fused_computation.30 | convolution fusion | flops 603979776 | bytes 10633216 | tf_op jit(solution)/shard_map/dot_general | solution.py:21
  15.0 63.0 %all-reduce.9 = bf16[64,576]{1,0:T(8,128)(2,1)S(1)} all-reduce(f32[64,576]{1,0:T(8,128)S(1)} %fusion.16), channel_id=1, replica_groups=mesh['samp'=16,'feat'=16] {'feat'}, use_global_device_ids=true, to_apply=%region_0.0 | all-reduce | flops 36864 | bytes 221184 | tf_op jit(solution)/shard_map/psum | solution.py:24
  77.9 6.9 %fusion.21 = f32[64,8192]{1,0:T(8,128)} fusion(bf16[64,576]{1,0:T(8,128)(2,1)S(1)} %all-reduce.9, bf16[576,8192]{1,0:T(8,128)(2,1)} %param.5), kind=kOutput, calls=%fused_computation.35 | convolution fusion | flops 603979776 | bytes 11608064 | tf_op jit(solution)/shard_map/dot_general | solution.py:25
  84.9 0.0 all-reduce.6.cloned.1.call-update
  84.9 0.0 all-reduce.8.cloned.1.call-start
  84.9 127.8 %all-reduce.6.cloned.1.call-done = f32[64,8192]{1,0:T(8,128)} async-done(((f32[64,8192]{1,0:T(8,128)}), f32[64,8192]{1,0:T(8,128)}) %all-reduce.6.cloned.1.call-update) | async-done | bytes 2097168 | tf_op jit(solution)/shard_map/psum | solution.py:26
  212.7 0.0 copy-start.2
  212.7 4.2 fusion.17
  216.9 60.3 %psum.58 = f32[64,64]{0,1:T(8,128)S(1)} all-reduce(f32[64,64]{0,1:T(8,128)S(1)} %fusion.17), channel_id=1, replica_groups=mesh['samp'=16,'feat'=16] {'feat'}, use_global_device_ids=true, to_apply=%region_2.0 | all-reduce | flops 4096 | bytes 32768 | tf_op jit(solution)/shard_map/psum | solution.py:28
  277.1 0.1 copy.5
  277.2 5.8 cholesky.44
  283.1 0.6 compare_reduce_fusion.1
  283.8 0.7 fusion.7
  284.4 4.9 custom-call.6
  289.3 0.0 copy-done.2
  289.3 1.9 convolution_convert_fusion
  291.2 6.6 %fusion.18 = f32[64,576]{1,0:T(8,128)S(1)} fusion(bf16[64,8192]{1,0:T(8,128)(2,1)S(1)} %convolution_convert_fusion, bf16[576,8192]{1,0:T(8,128)(2,1)} %param.5), kind=kOutput, calls=%fused_computation.32 | convolution fusion | flops 603979776 | bytes 10633216 | tf_op jit(solution)/shard_map/dot_general | solution.py:21
  297.8 57.4 %all-reduce.10 = bf16[64,576]{1,0:T(8,128)(2,1)S(1)} all-reduce(f32[64,576]{1,0:T(8,128)S(1)} %fusion.18), channel_id=1, replica_groups=mesh['samp'=16,'feat'=16] {'feat'}, use_global_device_ids=true, to_apply=%region_5.8 | all-reduce | flops 36864 | bytes 221184 | tf_op jit(solution)/shard_map/psum | solution.py:24
  355.3 6.9 %fusion.20 = f32[64,8192]{1,0:T(8,128)} fusion(bf16[64,576]{1,0:T(8,128)(2,1)S(1)} %all-reduce.10, bf16[576,8192]{1,0:T(8,128)(2,1)} %param.5), kind=kOutput, calls=%fused_computation.34 | convolution fusion | flops 603979776 | bytes 11608064 | tf_op jit(solution)/shard_map/dot_general | solution.py:25
  362.2 0.0 all-reduce.8.cloned.1.call-update
  362.2 9.1 %fusion = f32[]{:T(128)} fusion(bf16[576,8192]{1,0:T(8,128)(2,1)} %param.5), kind=kLoop, calls=%fused_computation.1 | loop fusion | flops 14155775 | bytes 9437188 | tf_op jit(solution)/shard_map/sjw,sjw->j/dot_general | solution.py:38
  371.4 130.6 %all-reduce.8.cloned.1.call-done = f32[64,8192]{1,0:T(8,128)} async-done(((f32[64,8192]{1,0:T(8,128)}), f32[64,8192]{1,0:T(8,128)}) %all-reduce.8.cloned.1.call-update) | async-done | bytes 2097168 | tf_op jit(solution)/shard_map/psum | solution.py:26
  502.0 0.0 copy-start.1
  502.0 4.2 fusion.19
  506.1 60.3 %psum.61 = f32[64,64]{0,1:T(8,128)S(1)} all-reduce(f32[64,64]{0,1:T(8,128)S(1)} %fusion.19), channel_id=1, replica_groups=mesh['samp'=16,'feat'=16] {'feat'}, use_global_device_ids=true, to_apply=%region_7.10 | all-reduce | flops 4096 | bytes 32768 | tf_op jit(solution)/shard_map/psum | solution.py:28
  566.4 0.1 copy.7
  566.5 5.8 cholesky.55
  572.4 0.6 compare_reduce_fusion
  573.0 0.7 fusion.8
  573.7 4.9 custom-call.7
  578.6 0.0 copy-done.1
  578.6 3.3 broadcast_multiply_fusion
  581.9 6.7 %fusion.1 = f32[64]{0:T(128)S(1)} fusion(bf16[576,8192]{1,0:T(8,128)(2,1)} %param.5, bf16[64,8192]{1,0:T(8,128)(2,1)S(1)} %get-tuple-element.7), kind=kOutput, calls=%fused_computation.4 | convolution fusion | flops 604053440 | bytes 10486016 | tf_op jit(solution)/shard_map/kjw,sjw->jks/dot_general | solution.py:36
  588.6 38.4 %all-reduce = (f32[1,64]{1,0:T(1,128)S(1)}, f32[1]{0:T(128)}) all-reduce(f32[1,64]{1,0:T(1,128)S(1)} %bitcast.39, f32[1]{0:T(128)} %bitcast.7), channel_id=1, replica_groups=mesh['samp'=16,'feat'=16] {'samp'}, use_global_device_ids=true, to_apply=%region_9.12 | all-reduce | flops 65 | bytes 520 | tf_op jit(solution)/shard_map/psum | solution.py:39
  627.6 0.5 multiply_divide_fusion
  (4 shorter events, 0.1 us)
Async XLA Ops:
  7.2 1.2 copy-start
  7.2 205.5 %all-reduce.6.cloned.1.call-start = ((), (), s32[]{:S(2)}) async-start(), calls=%async_computation | async-start | bytes 4194304 | tf_op jit(solution)/shard_map/psum | solution.py:26
  84.9 417.1 %all-reduce.8.cloned.1.call-start = ((), (), s32[]{:S(2)}) async-start(), calls=%async_computation.1 | async-start | bytes 4194304 | tf_op jit(solution)/shard_map/psum | solution.py:26
  212.7 76.6 %copy-start.2 = (f32[64,8192]{1,0:T(8,128)S(1)}, f32[64,8192]{1,0:T(8,128)}, u32[]{:S(2)}) copy-start(f32[64,8192]{1,0:T(8,128)} %all-reduce.6.cloned.1.call-done) | copy-start | bytes 6291460
  502.0 76.6 %copy-start.1 = (f32[64,8192]{1,0:T(8,128)S(1)}, f32[64,8192]{1,0:T(8,128)}, u32[]{:S(2)}) copy-start(f32[64,8192]{1,0:T(8,128)} %all-reduce.8.cloned.1.call-done) | copy-start | bytes 6291460
Sparse Core Ops, SparseCore 0:
  85.0 127.6 all-reduce.5
  362.3 139.5 all-reduce.7
where the time goes:
time: 635 us
  blocking collectives  279 us (44%)
  waiting for transfers between devices  258 us (41%)
  matrix products  47.2 us (7%)
  other arithmetic  33.8 us (5%)
  between operations  14.8 us (2%)
    psum x2, waiting for transfers between devices, on_device(): pulled = lax.psum(partial_cols, 'samp')  258 us
    psum x2, blocking collectives, on_device(): gram = lax.psum(local_gram, 'feat')  121 us
    psum x2, blocking collectives, on_device(): projected = lax.psum(partial_rows, 'feat').astype(jnp.bfloat16)  120 us
    psum x1, blocking collectives, on_device(): captured, energy = lax.psum((captured, energy), 'samp')  38.4 us
    dot_general x2, matrix products, on_device(): jnp.dot(projected, differences, preferred_element_type=jnp.float32)  13.8 us
    dot_general x2, matrix products, on_device(): lax.dot_general(block, differences, (((1,), (1,)), ((), ())), preferred_e...  13.2 us
    another operation x6, other arithmetic, orthonormal(): lower = jnp.linalg.cholesky(gram)  13 us
  transfers between devices with their start and end apart: 2, of which 2 were waited for; matrix products, arithmetic and copies ran while one was open for 1% of the time, Pallas kernels for 0%

commit v1 on v0

--- a/solution.py
+++ b/solution.py
@@ -23,7 +23,7 @@
         )
         projected = lax.psum(partial_rows, "feat").astype(jnp.bfloat16)
         partial_cols = jnp.dot(projected, differences, preferred_element_type=jnp.float32)
-        pulled = lax.psum(partial_cols, "samp")
+        pulled = jnp.sum(lax.all_gather(partial_cols, "samp"), axis=0)
         local_gram = jnp.dot(pulled, pulled.T, precision=lax.Precision.HIGHEST)
         gram = lax.psum(local_gram, "feat")
         basis = orthonormal(pulled, gram)

time: 635 us -> 772 us (1.22)
  waiting for transfers between devices: 258 us -> 376 us
  other arithmetic: 33.8 us -> 57.3 us
    all_gather x0 -> x2, waiting for transfers between devices: none -> 376 us  [on_device(): pulled = jnp.sum(lax.all_gather(partial_cols, 'samp'), axis=0)]
    psum x2 -> x0, waiting for transfers between devices: 258 us -> none  [on_device(): pulled = lax.psum(partial_cols, 'samp')]
    reduce_sum x0 -> x2, other arithmetic: none -> 23.4 us  [on_device(): pulled = jnp.sum(lax.all_gather(partial_cols, 'samp'), axis=0)]
where the time goes in v1:
time: 772 us; the launch traced here: 771 us
  waiting for transfers between devices  376 us (49%)
  blocking collectives  279 us (36%)
  other arithmetic  57.3 us (7%)
  matrix products  42.5 us (6%)
  between operations  14.8 us (2%)
    all_gather x2, waiting for transfers between devices, on_device(): pulled = jnp.sum(lax.all_gather(partial_cols, 'samp'), axis=0)  376 us
    psum x2, blocking collectives, on_device(): gram = lax.psum(local_gram, 'feat')  121 us
    psum x2, blocking collectives, on_device(): projected = lax.psum(partial_rows, 'feat').astype(jnp.bfloat16)  120 us
    psum x1, blocking collectives, on_device(): captured, energy = lax.psum((captured, energy), 'samp')  37.5 us
    reduce_sum x2, other arithmetic, on_device(): pulled = jnp.sum(lax.all_gather(partial_cols, 'samp'), axis=0)  23.4 us
  transfers between devices with their start and end apart: 2, of which 2 were waited for; matrix products, arithmetic and copies ran while one was open for 1% of the time, Pallas kernels for 0%

profile of v1, /device:TPU:1, one launch (start us, length us, event | category | flops | bytes accessed | tf_op | source)
XLA Modules:
  0.0 771.0 jit_solution(3550830047695087890)
XLA Ops:
  7.2 0.0 copy-start
  7.2 0.0 all-gather.5.cloned.1.call-start
  7.2 1.2 copy-done
  8.4 6.6 fusion.16
  15.0 63.0 %all-reduce.3 = bf16[64,576]{1,0:T(8,128)(2,1)S(1)} all-reduce(f32[64,576]{1,0:T(8,128)S(1)} %fusion.16), channel_id=1, replica_groups=mesh['samp'=16,'feat'=16] {'feat'}, use_global_device_ids=true, to_apply=%region_0.0 | all-reduce | flops 36864 | bytes 221184 | tf_op jit(solution)/shard_map/psum | solution.py:24
  77.9 6.9 fusion.21
  84.9 0.0 all-gather.5.cloned.1.call-update
  84.9 0.0 all-gather.7.cloned.1.call-start
  84.9 187.9 %all-gather.5.cloned.1.call-done = f32[1024,8192]{1,0:T(8,128)} async-done(((f32[64,8192]{1,0:T(8,128)}), f32[1024,8192]{1,0:T(8,128)}) %all-gather.5.cloned.1.call-update) | async-done | bytes 33554448 | tf_op jit(solution)/shard_map/all_gather | solution.py:26
  272.8 11.7 %reduce_sum.29 = f32[64,8192]{1,0:T(8,128)S(1)} reduce(f32[16,64,8192]{2,1,0:T(8,128)} %bitcast.41, f32[]{:T(128)} %constant.34.clone.1), dimensions={0}, to_apply=%region_1.0 | reduce | flops 7864320 | bytes 35651588 | tf_op jit(solution)/shard_map/reduce_sum | solution.py:26
  284.5 1.8 fusion.17
  286.3 60.4 %psum.43 = f32[64,64]{0,1:T(8,128)S(1)} all-reduce(f32[64,64]{0,1:T(8,128)S(1)} %fusion.17), channel_id=1, replica_groups=mesh['samp'=16,'feat'=16] {'feat'}, use_global_device_ids=true, to_apply=%region_2.0 | all-reduce | flops 4096 | bytes 32768 | tf_op jit(solution)/shard_map/psum | solution.py:28
  346.7 0.1 copy.5
  346.8 5.8 cholesky.44
  352.7 0.6 compare_reduce_fusion.1
  353.3 0.7 fusion.7
  354.0 4.9 custom-call.6
  358.9 1.9 convolution_convert_fusion
  360.8 6.6 fusion.18
  367.4 57.4 %all-reduce.4 = bf16[64,576]{1,0:T(8,128)(2,1)S(1)} all-reduce(f32[64,576]{1,0:T(8,128)S(1)} %fusion.18), channel_id=1, replica_groups=mesh['samp'=16,'feat'=16] {'feat'}, use_global_device_ids=true, to_apply=%region_5.8 | all-reduce | flops 36864 | bytes 221184 | tf_op jit(solution)/shard_map/psum | solution.py:24
  424.9 6.9 fusion.20
  431.8 0.0 all-gather.7.cloned.1.call-update
  431.8 9.2 %fusion = f32[]{:T(128)} fusion(bf16[576,8192]{1,0:T(8,128)(2,1)} %param.5), kind=kLoop, calls=%fused_computation.1 | loop fusion | flops 14155775 | bytes 9437188 | tf_op jit(solution)/shard_map/sjw,sjw->j/dot_general | solution.py:38
  441.0 188.3 %all-gather.7.cloned.1.call-done = f32[1024,8192]{1,0:T(8,128)} async-done(((f32[64,8192]{1,0:T(8,128)}), f32[1024,8192]{1,0:T(8,128)}) %all-gather.7.cloned.1.call-update) | async-done | bytes 33554448 | tf_op jit(solution)/shard_map/all_gather | solution.py:26
  629.3 11.7 %reduce_sum.30 = f32[64,8192]{1,0:T(8,128)S(1)} reduce(f32[16,64,8192]{2,1,0:T(8,128)} %bitcast.42, f32[]{:T(128)} %constant.34.clone.1), dimensions={0}, to_apply=%region_6.9 | reduce | flops 7864320 | bytes 35651588 | tf_op jit(solution)/shard_map/reduce_sum | solution.py:26
  641.0 1.8 fusion.19
  642.8 60.4 %psum.45 = f32[64,64]{0,1:T(8,128)S(1)} all-reduce(f32[64,64]{0,1:T(8,128)S(1)} %fusion.19), channel_id=1, replica_groups=mesh['samp'=16,'feat'=16] {'feat'}, use_global_device_ids=true, to_apply=%region_7.10 | all-reduce | flops 4096 | bytes 32768 | tf_op jit(solution)/shard_map/psum | solution.py:28
  703.2 0.1 copy.7
  703.3 5.8 cholesky.55
  709.2 0.6 compare_reduce_fusion
  709.8 0.7 fusion.8
  710.5 4.9 custom-call.7
  715.4 3.3 broadcast_multiply_fusion
  718.7 0.0 copy-start.1
  718.7 6.8 fusion.1
  725.5 37.5 %all-reduce = (f32[1,64]{1,0:T(1,128)S(1)}, f32[1]{0:T(128)}) all-reduce(f32[1,64]{1,0:T(1,128)S(1)} %bitcast.43, f32[1]{0:T(128)} %bitcast.9), channel_id=1, replica_groups=mesh['samp'=16,'feat'=16] {'samp'}, use_global_device_ids=true, to_apply=%region_9.12 | all-reduce | flops 65 | bytes 520 | tf_op jit(solution)/shard_map/psum | solution.py:39
  763.7 0.5 multiply_divide_fusion
  764.2 0.0 copy-done.1
  (4 shorter events, 0.1 us)
Async XLA Ops:
  7.2 1.2 copy-start
  7.2 265.6 %all-gather.5.cloned.1.call-start = ((), (), s32[]{:S(2)}) async-start(), calls=%async_computation | async-start | bytes 35651584 | tf_op jit(solution)/shard_map/all_gather | solution.py:26
  84.9 544.4 %all-gather.7.cloned.1.call-start = ((), (), s32[]{:S(2)}) async-start(), calls=%async_computation.1 | async-start | bytes 35651584 | tf_op jit(solution)/shard_map/all_gather | solution.py:26
  718.7 45.5 %copy-start.1 = (bf16[64,8192]{1,0:T(8,128)(2,1)S(1)}, bf16[64,8192]{1,0:T(8,128)(2,1)}, u32[]{:S(2)}) copy-start(bf16[64,8192]{1,0:T(8,128)(2,1)} %param.6) | copy-start | bytes 3145732
Sparse Core Ops, SparseCore 0:
  85.0 187.7 all-gather.4
  431.9 197.3 all-gather.6
